TPU v7x, 32 devices: a whole 2x2x4 slice. The times are simulated.
32 devices in a mesh: mem: 4 (over z), gx: 4 (over y, core), gy: 2 (over x).
Axes of the slice: x: 2, y: 2, z: 4, core: 2. Of those that a mesh axis runs over, the one named last changes fastest.
Arguments:
- height: float32 [4, 4, 128, 256], P('mem', None, 'gx', 'gy'), may hold values from -4 to 4
- wind: float32 [4, 2, 4, 128, 256], P('mem', None, None, 'gx', 'gy'), may hold values from -0.8 to 0.8
- moisture: float32 [4, 4, 128, 256], P('mem', None, 'gx', 'gy'), may hold values from 0 to 2
- coeffs: float32 [4, 4, 4, 16384], P('mem', None, None, ('gx', 'gy')), may hold values from -6 to 6
- damping: float32 [16384], P(('gx', 'gy')), may hold values from 0.3 to 1
- vmix: float32 [4, 4], replicated, may hold values from -3 to 3
- basis: bfloat16 [16384, 384], P(('gx', 'gy')), may hold values from -0.046875 to 0.046875
- edge_source: int32 [768], replicated, may hold values from 0 to 383
- row_cell: int32 [128], replicated, may hold values from 0 to 15, never falling along the last dimension, each value on 1 to 16 neighbouring positions
- col_cell: int32 [256], replicated, may hold values from 0 to 31, never falling along the last dimension, each value on 1 to 16 neighbouring positions
- cond_rate: float32 [4], replicated, may hold values from 0.05 to 0.5
- saturation: float32 [4], replicated, may hold values from 0.5 to 1.5
- ancestry: int32 [4], replicated, may hold values from 0 to 3
Outputs:
- height_out: float32 [4, 4, 128, 256], P('mem', None, 'gx', 'gy')
- wind_out: float32 [4, 2, 4, 128, 256], P('mem', None, None, 'gx', 'gy')
- moisture_out: float32 [4, 4, 128, 256], P('mem', None, 'gx', 'gy')
- rainfall: float32 [4, 128, 256], P('mem', 'gx', 'gy')
- restricted: float32 [4, 4, 16, 32], P('mem')
- coeffs_out: float32 [4, 4, 4, 16384], P('mem', None, None, ('gx', 'gy'))
Inputs may be any that keep to these rules, and one draw needn't show every extreme that they name: row_cell never falls, and each of the 16 global rows holds 1 to 16 nest rows, one exactly 16. col_cell never falls, and each of the 32 global columns holds 1 to 16 nest columns, one exactly 16.
All inputs are finite; a program needn't handle non-finite values.
Results may differ from a plain program's by a relative error of at most 0.00035.
Values sent between devices are 32-bit elements; how exact they have to be, the bound alone decides.
A program may use at most 64 MiB of HBM per device.

v0:
```python
import jax
import jax.numpy as jnp
from jax import lax
from jax.sharding import PartitionSpec as P

RATIO = 8
ACOUSTIC = 2


acoustic_substep = 0.2
drift_step = 0.4


def extended(block, sides, width):
    for axis, dim in sides:
        count = lax.axis_size(axis)
        forward = [(i, i + 1) for i in range(count - 1)]
        backward = [(target, source) for source, target in forward]
        low = lax.ppermute(
            lax.slice_in_dim(block, block.shape[dim] - width, None, axis=dim), axis, forward
        )
        high = lax.ppermute(lax.slice_in_dim(block, 0, width, axis=dim), axis, backward)
        block = jnp.concatenate([low, block, high], axis=dim)
    return block


def side_values(rim, indices, rim_points, levels):
    table = (indices[None, :] == lax.iota(jnp.int32, rim_points)[:, None]).astype(jnp.float32)
    return jnp.dot(rim, table, precision=lax.Precision.HIGHEST).reshape(4, levels, indices.shape[0])


def frame(padded, sides, flags):
    western_edge, eastern_edge, southern_edge, northern_edge = sides
    at_west, at_east, at_south, at_north = flags
    size_x = padded.shape[2] - 2
    size_y = padded.shape[3] - 2
    current = padded[:, :, 0, 1 : 1 + size_y]
    padded = padded.at[:, :, 0, 1 : 1 + size_y].set(jnp.where(at_west, western_edge, current))
    current = padded[:, :, 1 + size_x, 1 : 1 + size_y]
    padded = padded.at[:, :, 1 + size_x, 1 : 1 + size_y].set(
        jnp.where(at_east, eastern_edge, current)
    )
    current = padded[:, :, 1 : 1 + size_x, 0]
    padded = padded.at[:, :, 1 : 1 + size_x, 0].set(jnp.where(at_south, southern_edge, current))
    current = padded[:, :, 1 : 1 + size_x, 1 + size_y]
    padded = padded.at[:, :, 1 : 1 + size_x, 1 + size_y].set(
        jnp.where(at_north, northern_edge, current)
    )
    return padded


def pick_sides(sides, first, last):
    return tuple((side[first:last] for side in sides))


def body(
    height,
    wind,
    moisture,
    coeffs,
    damping,
    vmix,
    basis,
    edge_source,
    row_cell,
    col_cell,
    cond_rate,
    saturation,
    ancestry,
):
    levels = height.shape[1]
    size_x = height.shape[2]
    size_y = height.shape[3]
    full_x = row_cell.shape[0]
    full_y = col_cell.shape[0]
    rim_points = basis.shape[1]
    row_index = lax.axis_index("gx")
    col_index = lax.axis_index("gy")
    row_start = row_index * size_x
    col_start = col_index * size_y
    coeff_new = jnp.einsum("lj,mfjk->mflk", vmix, coeffs, precision=lax.Precision.HIGHEST) * damping
    coeff_low = coeff_new.astype(jnp.bfloat16).reshape(4 * levels, -1)
    rim_part = jnp.dot(coeff_low, basis, preferred_element_type=jnp.float32)
    rim = lax.psum(rim_part, ("gx", "gy"))
    western_edge = side_values(
        rim, lax.dynamic_slice_in_dim(edge_source, col_start, size_y), rim_points, levels
    )
    eastern_edge = side_values(
        rim, lax.dynamic_slice_in_dim(edge_source, full_y + col_start, size_y), rim_points, levels
    )
    southern_edge = side_values(
        rim,
        lax.dynamic_slice_in_dim(edge_source, 2 * full_y + row_start, size_x),
        rim_points,
        levels,
    )
    northern_edge = side_values(
        rim,
        lax.dynamic_slice_in_dim(edge_source, 2 * full_y + full_x + row_start, size_x),
        rim_points,
        levels,
    )
    sides = (western_edge, eastern_edge, southern_edge, northern_edge)
    flags = (
        row_index == 0,
        row_index == lax.axis_size("gx") - 1,
        col_index == 0,
        col_index == lax.axis_size("gy") - 1,
    )
    h_field = height[0]
    u_field = wind[0, 0]
    v_field = wind[0, 1]
    q_field = moisture[0]
    for substep in range(ACOUSTIC):
        h_pad = extended(h_field[None], (("gx", 2), ("gy", 3)), 1)
        h_pad = frame(h_pad, pick_sides(sides, 0, 1), flags)[0]
        u_field = u_field - acoustic_substep * (h_pad[:, 2:, 1:-1] - h_pad[:, :-2, 1:-1])
        v_field = v_field - acoustic_substep * (h_pad[:, 1:-1, 2:] - h_pad[:, 1:-1, :-2])
        wind_pad = extended(jnp.stack([u_field, v_field]), (("gx", 2), ("gy", 3)), 1)
        wind_pad = frame(wind_pad, pick_sides(sides, 1, 3), flags)
        u_pad = wind_pad[0]
        v_pad = wind_pad[1]
        h_field = h_field - acoustic_substep * (
            u_pad[:, 2:, 1:-1] - u_pad[:, :-2, 1:-1] + (v_pad[:, 1:-1, 2:] - v_pad[:, 1:-1, :-2])
        )
    q_pad = extended(q_field[None], (("gx", 2), ("gy", 3)), 1)
    q_pad = frame(q_pad, pick_sides(sides, 3, 4), flags)[0]
    flux = (
        jnp.maximum(u_field, 0.0) * (q_field - q_pad[:, :-2, 1:-1])
        + jnp.minimum(u_field, 0.0) * (q_pad[:, 2:, 1:-1] - q_field)
        + (
            jnp.maximum(v_field, 0.0) * (q_field - q_pad[:, 1:-1, :-2])
            + jnp.minimum(v_field, 0.0) * (q_pad[:, 1:-1, 2:] - q_field)
        )
    )
    q_field = q_field - drift_step * flux
    excess = jnp.maximum(q_field - saturation[:, None, None], 0.0)
    fallen = cond_rate[:, None, None] * excess
    q_field = q_field - fallen
    rain = jnp.sum(fallen, axis=0)
    coarse_rows = full_x // RATIO
    coarse_cols = full_y // RATIO
    row_table = (row_cell[None, :] == lax.iota(jnp.int32, coarse_rows)[:, None]).astype(jnp.float32)
    col_table = (col_cell[None, :] == lax.iota(jnp.int32, coarse_cols)[:, None]).astype(jnp.float32)
    row_count = jnp.sum(row_table, axis=1)
    col_count = jnp.sum(col_table, axis=1)
    local_rows = lax.dynamic_slice_in_dim(row_table, row_start, size_x, 1)
    local_cols = lax.dynamic_slice_in_dim(col_table, col_start, size_y, 1)
    partial_value = jnp.einsum("ax,lxy->lay", local_rows, q_field, precision=lax.Precision.HIGHEST)
    partial_value = jnp.einsum(
        "lay,by->lab", partial_value, local_cols, precision=lax.Precision.HIGHEST
    )
    sums = lax.psum(partial_value, "gy")
    sums = lax.psum(sums, "gx")
    coarse = sums / (row_count[:, None] * col_count[None, :])
    states = (
        h_field[None],
        jnp.stack([u_field, v_field])[None],
        q_field[None],
        rain[None],
        coarse[None],
        coeff_new,
    )
    member_here = lax.axis_index("mem")
    everyone = (
        lax.all_gather(states[0], "mem", axis=0, tiled=True),
        lax.all_gather(states[1], "mem", axis=0, tiled=True),
        lax.all_gather(states[2], "mem", axis=0, tiled=True),
        lax.all_gather(states[3], "mem", axis=0, tiled=True),
        lax.all_gather(states[4], "mem", axis=0, tiled=True),
        lax.all_gather(states[5], "mem", axis=0, tiled=True),
    )
    source = ancestry[member_here]
    cloned = tuple(
        (lax.dynamic_index_in_dim(whole, source, 0, keepdims=True) for whole in everyone)
    )
    return (cloned[0], cloned[1], cloned[2], cloned[3], cloned[4], cloned[5])


def solution(mesh):
    in_specs = (
        P("mem", None, "gx", "gy"),
        P("mem", None, None, "gx", "gy"),
        P("mem", None, "gx", "gy"),
        P("mem", None, None, ("gx", "gy")),
        P(("gx", "gy")),
        P(),
        P(("gx", "gy"), None),
        P(),
        P(),
        P(),
        P(),
        P(),
        P(),
    )
    out_specs = (
        P("mem", None, "gx", "gy"),
        P("mem", None, None, "gx", "gy"),
        P("mem", None, "gx", "gy"),
        P("mem", "gx", "gy"),
        P("mem", None, None, None),
        P("mem", None, None, ("gx", "gy")),
    )
    return jax.shard_map(body, mesh=mesh, in_specs=in_specs, out_specs=out_specs, check_vma=False)
```

profile of v0, /device:TPU:0, one launch (start us, length us, event | category | flops | bytes accessed | tf_op | source)
XLA Modules:
  0.0 245.3 jit_solution(11485259475965265100)
XLA Ops:
  0.7 0.9 fusion.73
  1.5 2.4 collective-permute-start
  3.9 1.3 collective-permute-start.1
  5.2 0.7 fusion.71
  6.0 5.1 %collective-permute-start.16 = (f32[1,4,1,128]{3,1,2,0:T(4,128)S(1)}, f32[1,4,1,128]{3,1,2,0:T(4,128)S(1)}, u32[]{:S(2)}, u32[]{:S(2)}) collective-permute-start(f32[1,4,1,128]{3,1,2,0:T(4,128)S(1)} %copy.119), channel_id=1, source_target_pairs={{0,2},{2,4},{4,6},{1,3},{3,5},{5,7},{8,10},{10,12},{12,14},{9,11},... | collective-permute-start | bytes 6152 | tf_op jit(solution)/shard_map/ppermute | solution.py:19
  11.1 1.3 collective-permute-start.17
  12.5 1.2 dynamic_slice.48
  15.0 0.7 iota_compare_fusion.8
  15.7 0.8 convert_reduce_fusion
  16.5 0.7 iota_compare_fusion.9
  17.1 0.8 convert_reduce_fusion.1
  17.9 1.3 fusion.77
  19.6 25.8 %psum.21 = f32[16,384]{1,0:T(8,128)S(1)} all-reduce(f32[16,384]{1,0:T(8,128)S(1)} %fusion.78), channel_id=1, replica_groups=mesh['mem'=4,'gx'=4,'gy'=2] {'gx','gy'}, use_global_device_ids=true, to_apply=%region_0.0 | all-reduce | flops 6144 | bytes 49152 | tf_op jit(solution)/shard_map/psum | solution.py:84
  46.3 16.0 %all_gather.23 = f32[4,4,4,2048]{3,2,1,0:T(4,128)S(1)} all-gather(f32[1,4,4,2048]{3,2,1,0:T(4,128)S(1)} %get-tuple-element.293), channel_id=1, replica_groups=mesh['mem'=4,'gx'=4,'gy'=2] {'mem'}, dimensions={0}, use_global_device_ids=true | all-gather | bytes 655360 | tf_op jit(solution)/shard_map/all_gather | solution.py:171
  63.0 0.7 constant_dynamic-slice_fusion
  63.7 0.6 fusion.76
  64.8 1.3 collective-permute-start.3
  66.1 4.5 %collective-permute-start.2 = (f32[1,4,34,1]{3,1,2,0:T(4,128)S(1)}, f32[1,4,34,1]{3,1,2,0:T(4,128)S(1)}, u32[]{:S(2)}, u32[]{:S(2)}) collective-permute-start(f32[1,4,34,1]{3,1,2,0:T(4,128)S(1)} %get-tuple-element.270), channel_id=1, source_target_pairs={{0,1},{2,3},{4,5},{6,7},{8,9},{10,11},{12,13},{14,15},{16,17},{18,... | collective-permute-start | bytes 1640 | tf_op jit(solution)/shard_map/ppermute | solution.py:19
  71.0 1.6 collective-permute-done.2
  72.8 1.5 scatter.66
  75.3 2.4 scatter.71
  77.9 1.3 collective-permute-start.5
  79.2 3.0 %collective-permute-start.4 = (f32[2,4,1,128]{3,1,2,0:T(4,128)S(1)}, f32[2,4,1,128]{3,1,2,0:T(4,128)S(1)}, u32[]{:S(2)}, u32[]{:S(2)}) collective-permute-start(f32[2,4,1,128]{3,1,2,0:T(4,128)S(1)} %get-tuple-element.262), channel_id=1, source_target_pairs={{0,2},{2,4},{4,6},{1,3},{3,5},{5,7},{8,10},{10,12},{12,14},{9,11},... | collective-permute-start | bytes 12296 | tf_op jit(solution)/shard_map/ppermute | solution.py:19
  82.4 1.3 collective-permute-start.19
  83.7 4.5 %collective-permute-start.18 = (f32[1,4,34,1]{3,1,2,0:T(4,128)S(1)}, f32[1,4,34,1]{3,1,2,0:T(4,128)S(1)}, u32[]{:S(2)}, u32[]{:S(2)}) collective-permute-start(f32[1,4,34,1]{3,1,2,0:T(4,128)S(1)} %get-tuple-element.266), channel_id=1, source_target_pairs={{0,1},{2,3},{4,5},{6,7},{8,9},{10,11},{12,13},{14,15},{16,17},{18,... | collective-permute-start | bytes 1640 | tf_op jit(solution)/shard_map/ppermute | solution.py:19
  88.4 1.3 collective-permute-start.7
  89.7 4.6 %collective-permute-start.6 = (f32[2,4,34,1]{3,1,2,0:T(4,128)S(1)}, f32[2,4,34,1]{3,1,2,0:T(4,128)S(1)}, u32[]{:S(2)}, u32[]{:S(2)}) collective-permute-start(f32[2,4,34,1]{3,1,2,0:T(4,128)S(1)} %get-tuple-element.256), channel_id=1, source_target_pairs={{0,1},{2,3},{4,5},{6,7},{8,9},{10,11},{12,13},{14,15},{16,17},{18,... | collective-permute-start | bytes 3272 | tf_op jit(solution)/shard_map/ppermute | solution.py:19
  94.3 2.4 collective-permute-done.7
  96.7 1.5 collective-permute-done.6
  98.5 1.6 scatter.74
  100.3 0.4 scatter.75
  100.7 0.5 scatter.76
  101.3 4.8 %scatter.79 = f32[2,4,34,130]{3,1,2,0:T(4,128)S(1)} dynamic-update-slice(f32[2,4,34,130]{3,1,2,0:T(4,128)S(1)} %scatter.76, f32[2,4,32,1]{3,1,2,0:T(4,128)S(1)} %slice_select_fusion.2, s32[]{:T(128)} %constant.509.clone.1, s32[]{:T(128)} %constant.509.clone.1, s32[]{:T(128)} %constant.516.clone.1, s32[]{:T(128)} %constant.522.clone.1) | dynamic-update-slice | bytes 2052 | tf_op jit(solution)/shard_map/scatter | solution.py:46
  106.3 1.9 collective-permute-start.8
  108.2 1.3 collective-permute-start.9
  109.8 1.9 collective-permute-done.9
  111.7 1.3 collective-permute-start.11
  113.0 4.5 %collective-permute-start.10 = (f32[1,4,34,1]{3,1,2,0:T(4,128)S(1)}, f32[1,4,34,1]{3,1,2,0:T(4,128)S(1)}, u32[]{:S(2)}, u32[]{:S(2)}) collective-permute-start(f32[1,4,34,1]{3,1,2,0:T(4,128)S(1)} %get-tuple-element.268), channel_id=1, source_target_pairs={{0,1},{2,3},{4,5},{6,7},{8,9},{10,11},{12,13},{14,15},{16,17},{18,... | collective-permute-start | bytes 1640 | tf_op jit(solution)/shard_map/ppermute | solution.py:19
  117.6 1.5 scatter.94
  119.1 0.4 collective-permute-done.10
  119.7 1.5 scatter.80
  123.3 2.4 scatter.99
  125.7 2.6 %scatter.85 = f32[4,34,130]{2,0,1:T(4,128)S(1)} dynamic-update-slice(f32[4,34,130]{2,0,1:T(4,128)S(1)} %bitcast.149, f32[4,32,1]{2,0,1:T(4,128)S(1)} %copy.88, s32[]{:T(128)} %constant.509.clone.1, s32[]{:T(128)} %constant.516.clone.1, s32[]{:T(128)} %constant.522.clone.1) | dynamic-update-slice | bytes 1028 | tf_op jit(solution)/shard_map/scatter | solution.py:46
  128.7 1.3 collective-permute-start.13
  130.0 4.0 %collective-permute-start.12 = (f32[2,4,1,128]{3,1,2,0:T(4,128)S(1)}, f32[2,4,1,128]{3,1,2,0:T(4,128)S(1)}, u32[]{:S(2)}, u32[]{:S(2)}) collective-permute-start(f32[2,4,1,128]{3,1,2,0:T(4,128)S(1)} %get-tuple-element.260), channel_id=1, source_target_pairs={{0,2},{2,4},{4,6},{1,3},{3,5},{5,7},{8,10},{10,12},{12,14},{9,11},... | collective-permute-start | bytes 12296 | tf_op jit(solution)/shard_map/ppermute | solution.py:19
  134.0 17.0 %all-gather.1 = f32[8,4,32,128]{3,2,1,0:T(8,128)S(1)} all-gather(f32[2,4,32,128]{3,2,1,0:T(8,128)S(1)} %copy.92), channel_id=3, replica_groups=mesh['mem'=4,'gx'=4,'gy'=2] {'mem'}, dimensions={0}, use_global_device_ids=true | all-gather | bytes 655360 | tf_op jit(solution)/shard_map/all_gather | solution.py:167
  151.0 0.7 constant_dynamic-slice_fusion.4
  151.8 13.9 %all-gather.2 = f32[16,32,128]{2,1,0:T(8,128)S(1)} all-gather(f32[4,32,128]{2,1,0:T(8,128)S(1)} %copy.101), channel_id=4, replica_groups=mesh['mem'=4,'gx'=4,'gy'=2] {'mem'}, dimensions={0}, use_global_device_ids=true | all-gather | bytes 327680 | tf_op jit(solution)/shard_map/all_gather | solution.py:168
  165.7 0.6 constant_dynamic-slice_fusion.3
  166.4 13.1 %all-gather.3 = f32[128,128]{1,0:T(8,128)S(1)} all-gather(f32[32,128]{1,0:T(8,128)S(1)} %get-tuple-element.246), channel_id=5, replica_groups=mesh['mem'=4,'gx'=4,'gy'=2] {'mem'}, dimensions={0}, use_global_device_ids=true | all-gather | bytes 81920 | tf_op jit(solution)/shard_map/all_gather | solution.py:169
  179.8 8.8 %psum.22 = f32[4,16,32]{2,1,0:T(8,128)S(1)} all-reduce(f32[4,16,32]{2,1,0:T(8,128)S(1)} %fusion.36), channel_id=1, replica_groups=mesh['mem'=4,'gx'=4,'gy'=2] {'gy'}, use_global_device_ids=true, to_apply=%region_2.3 | all-reduce | flops 2048 | bytes 16384 | tf_op jit(solution)/shard_map/psum | solution.py:153
  188.6 10.3 %psum.23 = f32[4,16,32]{2,1,0:T(8,128)S(1)} all-reduce(f32[4,16,32]{2,1,0:T(8,128)S(1)} %psum.22), channel_id=1, replica_groups=mesh['mem'=4,'gx'=4,'gy'=2] {'gx'}, use_global_device_ids=true, to_apply=%region_3.4 | all-reduce | flops 2048 | bytes 16384 | tf_op jit(solution)/shard_map/psum | solution.py:154
  198.9 13.4 %all-gather.4 = f32[16,16,32]{2,1,0:T(8,128)S(1)} all-gather(f32[4,16,32]{2,1,0:T(8,128)S(1)} %broadcast_divide_fusion), channel_id=6, replica_groups=mesh['mem'=4,'gx'=4,'gy'=2] {'mem'}, dimensions={0}, use_global_device_ids=true | all-gather | bytes 40960 | tf_op jit(solution)/shard_map/all_gather | solution.py:170
  212.3 0.6 constant_dynamic-slice_fusion.1
  212.9 0.6 constant_dynamic-slice_fusion.2
  213.7 1.3 collective-permute-start.15
  215.0 4.6 %collective-permute-start.14 = (f32[2,4,34,1]{3,1,2,0:T(4,128)S(1)}, f32[2,4,34,1]{3,1,2,0:T(4,128)S(1)}, u32[]{:S(2)}, u32[]{:S(2)}) collective-permute-start(f32[2,4,34,1]{3,1,2,0:T(4,128)S(1)} %get-tuple-element.254), channel_id=1, source_target_pairs={{0,1},{2,3},{4,5},{6,7},{8,9},{10,11},{12,13},{14,15},{16,17},{18,... | collective-permute-start | bytes 3272 | tf_op jit(solution)/shard_map/ppermute | solution.py:19
  219.6 1.1 collective-permute-done.15
  220.6 1.5 collective-permute-done.14
  222.4 1.6 scatter.86
  224.6 0.5 scatter.90
  225.2 4.8 %scatter.91 = f32[2,4,34,130]{3,1,2,0:T(4,128)S(1)} dynamic-update-slice(f32[2,4,34,130]{3,1,2,0:T(4,128)S(1)} %scatter.90, f32[2,4,32,1]{3,1,2,0:T(4,128)S(1)} %slice_select_fusion, s32[]{:T(128)} %constant.509.clone.1, s32[]{:T(128)} %constant.509.clone.1, s32[]{:T(128)} %constant.516.clone.1, s32[]{:T(128)} %constant.522.clone.1) | dynamic-update-slice | bytes 2052 | tf_op jit(solution)/shard_map/scatter | solution.py:46
  230.2 14.5 %all-gather = f32[16,32,128]{2,1,0:T(8,128)S(1)} all-gather(f32[4,32,128]{2,1,0:T(8,128)S(1)} %copy.91), channel_id=2, replica_groups=mesh['mem'=4,'gx'=4,'gy'=2] {'mem'}, dimensions={0}, use_global_device_ids=true | all-gather | bytes 327680 | tf_op jit(solution)/shard_map/all_gather | solution.py:166
  244.6 0.6 constant_dynamic-slice_fusion.5
  (125 shorter events, 9.2 us)
Async XLA Ops:
  0.6 18.6 %copy-start = (bf16[2048,384]{1,0:T(8,128)(2,1)S(1)}, bf16[2048,384]{1,0:T(8,128)(2,1)}, u32[]{:S(2)}) copy-start(bf16[2048,384]{1,0:T(8,128)(2,1)} %param.59) | copy-start | bytes 4718596
  0.6 44.7 %copy-start.6 = (s32[768]{0:T(1024)S(1)}, s32[768]{0:T(1024)}, u32[]{:S(2)}) copy-start(s32[768]{0:T(1024)} %param.60) | copy-start | bytes 9220
  0.7 45.6 %copy-start.3 = (f32[1,2,4,32,128]{4,3,2,1,0:T(8,128)S(1)}, f32[1,2,4,32,128]{4,3,2,1,0:T(8,128)}, u32[]{:S(2)}) copy-start(f32[1,2,4,32,128]{4,3,2,1,0:T(8,128)} %param.54) | copy-start | bytes 393220
  1.5 63.1 %collective-permute-start = (f32[1,4,1,128]{3,1,2,0:T(4,128)S(1)}, f32[1,4,1,128]{3,1,2,0:T(4,128)S(1)}, u32[]{:S(2)}, u32[]{:S(2)}) collective-permute-start(f32[1,4,1,128]{3,1,2,0:T(4,128)S(1)} %copy.117), channel_id=1, source_target_pairs={{0,2},{2,4},{4,6},{1,3},{3,5},{5,7},{8,10},{10,12},{12,14},{9,11},... | collective-permute-start | bytes 6152 | tf_op jit(solution)/shard_map/ppermute | solution.py:19
  3.9 60.7 %collective-permute-start.1 = (f32[1,4,1,128]{3,1,2,0:T(4,128)S(1)}, f32[1,4,1,128]{3,1,2,0:T(4,128)S(1)}, u32[]{:S(2)}, u32[]{:S(2)}) collective-permute-start(f32[1,4,1,128]{3,1,2,0:T(4,128)S(1)} %copy.118), channel_id=1, source_target_pairs={{2,0},{4,2},{6,4},{3,1},{5,3},{7,5},{10,8},{12,10},{14,12},{11,9},... | collective-permute-start | bytes 6152 | tf_op jit(solution)/shard_map/ppermute | solution.py:22
  6.0 64.7 %collective-permute-start.16 = (f32[1,4,1,128]{3,1,2,0:T(4,128)S(1)}, f32[1,4,1,128]{3,1,2,0:T(4,128)S(1)}, u32[]{:S(2)}, u32[]{:S(2)}) collective-permute-start(f32[1,4,1,128]{3,1,2,0:T(4,128)S(1)} %copy.119), channel_id=1, source_target_pairs={{0,2},{2,4},{4,6},{1,3},{3,5},{5,7},{8,10},{10,12},{12,14},{9,11},... | collective-permute-start | bytes 6152 | tf_op jit(solution)/shard_map/ppermute | solution.py:19
  11.1 59.6 %collective-permute-start.17 = (f32[1,4,1,128]{3,1,2,0:T(4,128)S(1)}, f32[1,4,1,128]{3,1,2,0:T(4,128)S(1)}, u32[]{:S(2)}, u32[]{:S(2)}) collective-permute-start(f32[1,4,1,128]{3,1,2,0:T(4,128)S(1)} %copy.120), channel_id=1, source_target_pairs={{2,0},{4,2},{6,4},{3,1},{5,3},{7,5},{10,8},{12,10},{14,12},{11,9},... | collective-permute-start | bytes 6152 | tf_op jit(solution)/shard_map/ppermute | solution.py:22
  19.2 45.4 %copy-start.2 = (f32[1,4,32,128]{3,2,1,0:T(8,128)S(1)}, f32[1,4,32,128]{3,2,1,0:T(8,128)}, u32[]{:S(2)}) copy-start(f32[1,4,32,128]{3,2,1,0:T(8,128)} %param.53) | copy-start | bytes 196612
  19.2 51.4 %copy-start.1 = (f32[1,4,32,128]{3,2,1,0:T(8,128)S(1)}, f32[1,4,32,128]{3,2,1,0:T(8,128)}, u32[]{:S(2)}) copy-start(f32[1,4,32,128]{3,2,1,0:T(8,128)} %param.55) | copy-start | bytes 196612
  64.8 6.2 %collective-permute-start.3 = (f32[1,4,34,1]{3,1,2,0:T(4,128)S(1)}, f32[1,4,34,1]{3,1,2,0:T(4,128)S(1)}, u32[]{:S(2)}, u32[]{:S(2)}) collective-permute-start(f32[1,4,34,1]{3,1,2,0:T(4,128)S(1)} %get-tuple-element.271), channel_id=1, source_target_pairs={{1,0},{3,2},{5,4},{7,6},{9,8},{11,10},{13,12},{15,14},{17,16},{19,... | collective-permute-start | bytes 1640 | tf_op jit(solution)/shard_map/ppermute | solution.py:22
  66.1 6.5 %collective-permute-start.2 = (f32[1,4,34,1]{3,1,2,0:T(4,128)S(1)}, f32[1,4,34,1]{3,1,2,0:T(4,128)S(1)}, u32[]{:S(2)}, u32[]{:S(2)}) collective-permute-start(f32[1,4,34,1]{3,1,2,0:T(4,128)S(1)} %get-tuple-element.270), channel_id=1, source_target_pairs={{0,1},{2,3},{4,5},{6,7},{8,9},{10,11},{12,13},{14,15},{16,17},{18,... | collective-permute-start | bytes 1640 | tf_op jit(solution)/shard_map/ppermute | solution.py:19
  77.9 10.3 %collective-permute-start.5 = (f32[2,4,1,128]{3,1,2,0:T(4,128)S(1)}, f32[2,4,1,128]{3,1,2,0:T(4,128)S(1)}, u32[]{:S(2)}, u32[]{:S(2)}) collective-permute-start(f32[2,4,1,128]{3,1,2,0:T(4,128)S(1)} %get-tuple-element.263), channel_id=1, source_target_pairs={{2,0},{4,2},{6,4},{3,1},{5,3},{7,5},{10,8},{12,10},{14,12},{11,9},... | collective-permute-start | bytes 12296 | tf_op jit(solution)/shard_map/ppermute | solution.py:22
  79.2 9.0 %collective-permute-start.4 = (f32[2,4,1,128]{3,1,2,0:T(4,128)S(1)}, f32[2,4,1,128]{3,1,2,0:T(4,128)S(1)}, u32[]{:S(2)}, u32[]{:S(2)}) collective-permute-start(f32[2,4,1,128]{3,1,2,0:T(4,128)S(1)} %get-tuple-element.262), channel_id=1, source_target_pairs={{0,2},{2,4},{4,6},{1,3},{3,5},{5,7},{8,10},{10,12},{12,14},{9,11},... | collective-permute-start | bytes 12296 | tf_op jit(solution)/shard_map/ppermute | solution.py:19
  82.4 27.2 %collective-permute-start.19 = (f32[1,4,34,1]{3,1,2,0:T(4,128)S(1)}, f32[1,4,34,1]{3,1,2,0:T(4,128)S(1)}, u32[]{:S(2)}, u32[]{:S(2)}) collective-permute-start(f32[1,4,34,1]{3,1,2,0:T(4,128)S(1)} %get-tuple-element.267), channel_id=1, source_target_pairs={{1,0},{3,2},{5,4},{7,6},{9,8},{11,10},{13,12},{15,14},{17,16},{19,... | collective-permute-start | bytes 1640 | tf_op jit(solution)/shard_map/ppermute | solution.py:22
  83.7 25.9 %collective-permute-start.18 = (f32[1,4,34,1]{3,1,2,0:T(4,128)S(1)}, f32[1,4,34,1]{3,1,2,0:T(4,128)S(1)}, u32[]{:S(2)}, u32[]{:S(2)}) collective-permute-start(f32[1,4,34,1]{3,1,2,0:T(4,128)S(1)} %get-tuple-element.266), channel_id=1, source_target_pairs={{0,1},{2,3},{4,5},{6,7},{8,9},{10,11},{12,13},{14,15},{16,17},{18,... | collective-permute-start | bytes 1640 | tf_op jit(solution)/shard_map/ppermute | solution.py:19
  88.4 8.3 %collective-permute-start.7 = (f32[2,4,34,1]{3,1,2,0:T(4,128)S(1)}, f32[2,4,34,1]{3,1,2,0:T(4,128)S(1)}, u32[]{:S(2)}, u32[]{:S(2)}) collective-permute-start(f32[2,4,34,1]{3,1,2,0:T(4,128)S(1)} %get-tuple-element.257), channel_id=1, source_target_pairs={{1,0},{3,2},{5,4},{7,6},{9,8},{11,10},{13,12},{15,14},{17,16},{19,... | collective-permute-start | bytes 3272 | tf_op jit(solution)/shard_map/ppermute | solution.py:22
  89.7 8.5 %collective-permute-start.6 = (f32[2,4,34,1]{3,1,2,0:T(4,128)S(1)}, f32[2,4,34,1]{3,1,2,0:T(4,128)S(1)}, u32[]{:S(2)}, u32[]{:S(2)}) collective-permute-start(f32[2,4,34,1]{3,1,2,0:T(4,128)S(1)} %get-tuple-element.256), channel_id=1, source_target_pairs={{0,1},{2,3},{4,5},{6,7},{8,9},{10,11},{12,13},{14,15},{16,17},{18,... | collective-permute-start | bytes 3272 | tf_op jit(solution)/shard_map/ppermute | solution.py:19
  106.1 22.2 %copy-start.4 = (f32[4]{0:T(128)S(1)}, f32[4]{0:T(128)}, u32[]{:S(2)}) copy-start(f32[4]{0:T(128)} %param.64) | copy-start | bytes 52
  106.1 22.2 %copy-start.5 = (f32[4]{0:T(128)S(1)}, f32[4]{0:T(128)}, u32[]{:S(2)}) copy-start(f32[4]{0:T(128)} %param.63) | copy-start | bytes 52
  106.3 3.4 %collective-permute-start.8 = (f32[1,4,1,128]{3,1,2,0:T(4,128)S(1)}, f32[1,4,1,128]{3,1,2,0:T(4,128)S(1)}, u32[]{:S(2)}, u32[]{:S(2)}) collective-permute-start(f32[1,4,1,128]{3,1,2,0:T(4,128)S(1)} %get-tuple-element.274), channel_id=1, source_target_pairs={{0,2},{2,4},{4,6},{1,3},{3,5},{5,7},{8,10},{10,12},{12,14},{9,11},... | collective-permute-start | bytes 6152 | tf_op jit(solution)/shard_map/ppermute | solution.py:19
  108.2 3.4 %collective-permute-start.9 = (f32[1,4,1,128]{3,1,2,0:T(4,128)S(1)}, f32[1,4,1,128]{3,1,2,0:T(4,128)S(1)}, u32[]{:S(2)}, u32[]{:S(2)}) collective-permute-start(f32[1,4,1,128]{3,1,2,0:T(4,128)S(1)} %get-tuple-element.275), channel_id=1, source_target_pairs={{2,0},{4,2},{6,4},{3,1},{5,3},{7,5},{10,8},{12,10},{14,12},{11,9},... | collective-permute-start | bytes 6152 | tf_op jit(solution)/shard_map/ppermute | solution.py:22
  111.7 7.4 %collective-permute-start.11 = (f32[1,4,34,1]{3,1,2,0:T(4,128)S(1)}, f32[1,4,34,1]{3,1,2,0:T(4,128)S(1)}, u32[]{:S(2)}, u32[]{:S(2)}) collective-permute-start(f32[1,4,34,1]{3,1,2,0:T(4,128)S(1)} %get-tuple-element.269), channel_id=1, source_target_pairs={{1,0},{3,2},{5,4},{7,6},{9,8},{11,10},{13,12},{15,14},{17,16},{19,... | collective-permute-start | bytes 1640 | tf_op jit(solution)/shard_map/ppermute | solution.py:22
  113.0 6.5 %collective-permute-start.10 = (f32[1,4,34,1]{3,1,2,0:T(4,128)S(1)}, f32[1,4,34,1]{3,1,2,0:T(4,128)S(1)}, u32[]{:S(2)}, u32[]{:S(2)}) collective-permute-start(f32[1,4,34,1]{3,1,2,0:T(4,128)S(1)} %get-tuple-element.268), channel_id=1, source_target_pairs={{0,1},{2,3},{4,5},{6,7},{8,9},{10,11},{12,13},{14,15},{16,17},{18,... | collective-permute-start | bytes 1640 | tf_op jit(solution)/shard_map/ppermute | solution.py:19
  128.7 84.8 %collective-permute-start.13 = (f32[2,4,1,128]{3,1,2,0:T(4,128)S(1)}, f32[2,4,1,128]{3,1,2,0:T(4,128)S(1)}, u32[]{:S(2)}, u32[]{:S(2)}) collective-permute-start(f32[2,4,1,128]{3,1,2,0:T(4,128)S(1)} %get-tuple-element.261), channel_id=1, source_target_pairs={{2,0},{4,2},{6,4},{3,1},{5,3},{7,5},{10,8},{12,10},{14,12},{11,9},... | collective-permute-start | bytes 12296 | tf_op jit(solution)/shard_map/ppermute | solution.py:22
  130.0 83.5 %collective-permute-start.12 = (f32[2,4,1,128]{3,1,2,0:T(4,128)S(1)}, f32[2,4,1,128]{3,1,2,0:T(4,128)S(1)}, u32[]{:S(2)}, u32[]{:S(2)}) collective-permute-start(f32[2,4,1,128]{3,1,2,0:T(4,128)S(1)} %get-tuple-element.260), channel_id=1, source_target_pairs={{0,2},{2,4},{4,6},{1,3},{3,5},{5,7},{8,10},{10,12},{12,14},{9,11},... | collective-permute-start | bytes 12296 | tf_op jit(solution)/shard_map/ppermute | solution.py:19
  213.7 6.9 %collective-permute-start.15 = (f32[2,4,34,1]{3,1,2,0:T(4,128)S(1)}, f32[2,4,34,1]{3,1,2,0:T(4,128)S(1)}, u32[]{:S(2)}, u32[]{:S(2)}) collective-permute-start(f32[2,4,34,1]{3,1,2,0:T(4,128)S(1)} %get-tuple-element.255), channel_id=1, source_target_pairs={{1,0},{3,2},{5,4},{7,6},{9,8},{11,10},{13,12},{15,14},{17,16},{19,... | collective-permute-start | bytes 3272 | tf_op jit(solution)/shard_map/ppermute | solution.py:22
  215.0 7.1 %collective-permute-start.14 = (f32[2,4,34,1]{3,1,2,0:T(4,128)S(1)}, f32[2,4,34,1]{3,1,2,0:T(4,128)S(1)}, u32[]{:S(2)}, u32[]{:S(2)}) collective-permute-start(f32[2,4,34,1]{3,1,2,0:T(4,128)S(1)} %get-tuple-element.254), channel_id=1, source_target_pairs={{0,1},{2,3},{4,5},{6,7},{8,9},{10,11},{12,13},{14,15},{16,17},{18,... | collective-permute-start | bytes 3272 | tf_op jit(solution)/shard_map/ppermute | solution.py:19
where the time goes:
time: 246 us; the launch traced here: 245 us
  blocking collectives  133 us (54%)
  starting transfers between devices  52.2 us (21%)
  local copies, waits for them, and re-layouts  37.8 us (15%)
  waiting for transfers between devices  10.6 us (4%)
  other arithmetic  5.81 us (2%)
  between operations  3.52 us (1%)
  matrix products  2.68 us (1%)
    ppermute x10, starting transfers between devices, extended(): lax.ppermute(lax.slice_in_dim(block, block.shape[dim] - width, None, axis...  39.2 us
    psum x1, blocking collectives, body(): rim = lax.psum(rim_part, ('gx', 'gy'))  25.8 us
    all_gather x1, blocking collectives, body(): lax.all_gather(states[1], 'mem', axis=0, tiled=True)  17 us
    scatter x5, local copies, waits for them, and re-layouts, frame(): padded.at[:, :, 1:1 + size_x, 1 + size_y]  16.9 us
    all_gather x1, blocking collectives, body(): lax.all_gather(states[5], 'mem', axis=0, tiled=True)  16 us
    all_gather x1, blocking collectives, body(): lax.all_gather(states[0], 'mem', axis=0, tiled=True)  14.5 us
    all_gather x1, blocking collectives, body(): lax.all_gather(states[2], 'mem', axis=0, tiled=True)  13.9 us
    all_gather x1, blocking collectives, body(): lax.all_gather(states[4], 'mem', axis=0, tiled=True)  13.4 us
  transfers between devices with their start and end apart: 20, of which 8 were waited for; matrix products, arithmetic and copies ran while one was open for 9% of the time, Pallas kernels for 0%

commit v1 on v0

v1 whole, which is shorter than its diff:
```python
import functools

import jax
import jax.numpy as jnp
from jax import lax
from jax.experimental import pallas as pl
from jax.experimental.pallas import tpu as pltpu
from jax.sharding import PartitionSpec as P

RATIO = 8
ACOUSTIC = 2
HALO = 8

acoustic_substep = 0.2
drift_step = 0.4

MESH = pl.DeviceIdType.MESH


def kernel(
    sizes,
    height,
    wind,
    moisture,
    coeffs,
    damping,
    vmix,
    basis,
    edge_source,
    row_cell,
    col_cell,
    cond_rate,
    saturation,
    ancestry,
    height_out,
    wind_out,
    moisture_out,
    rain_out,
    coarse_out,
    coeffs_out,
    basis_buf,
    spec_a,
    spec_b,
    state_0,
    state_1,
    state_2,
    state_3,
    coarse_all,
    relay_spec,
    relay_state,
    relay_coarse,
    packed,
    packed_in,
    diag_in,
    rows_h,
    rows_w,
    rows_q,
    rim_part,
    rim_in,
    rim_full,
    table,
    sides,
    sides_t,
    coarse_rows_buf,
    coarse_part,
    coarse_in,
    basis_sem,
    halo_send,
    halo_recv,
    rim_send,
    rim_recv,
    rimg_send,
    rimg_recv,
    crs_send,
    crs_recv,
    mem_send,
    mem_recv,
):
    members, count_x, count_y = sizes
    plane = count_x * count_y
    levels = height.shape[1]
    size_x = height.shape[2]
    size_y = height.shape[3]
    full_x = row_cell.shape[1]
    full_y = col_cell.shape[1]
    rim_points = basis.shape[1]
    coarse_x = coarse_out.shape[2]
    coarse_y = coarse_out.shape[3]
    share = rim_part.shape[1]
    f32 = jnp.float32

    z = lax.axis_index("mem")
    ix = lax.axis_index("gx")
    iy = lax.axis_index("gy")
    here = ix * count_y + iy
    inner = jnp.logical_and(z > 0, z < members - 1)
    outer = jnp.logical_not(inner)
    across = jnp.where(z < 2, 2, 1)
    near = jnp.where(z < 2, 1, 2)
    outward = jnp.where(z < 2, 0, 3)

    fetch = pltpu.make_async_copy(basis, basis_buf, basis_sem)
    fetch.start()

    def plane_peer(step):
        other = lax.rem(here + step, plane)
        return other, other // count_y, lax.rem(other, count_y)

    barrier = pltpu.get_barrier_semaphore()
    for step in range(1, plane):
        _, px, py = plane_peer(step)
        pl.semaphore_signal(barrier, inc=1, device_id=(z, px, py), device_id_type=MESH)
    for step in range(1, members):
        pl.semaphore_signal(
            barrier,
            inc=1,
            device_id=(lax.rem(z + step, members), ix, iy),
            device_id_type=MESH,
        )

    new_fields = []
    for f in range(4):
        c = coeffs[0, f]
        acc = vmix[:, 0:1] * c[0:1]
        for j in range(1, levels):
            acc = acc + vmix[:, j : j + 1] * c[j : j + 1]
        new_fields.append(acc * damping[...])
    for f in range(4):
        buf = spec_a if f < 2 else spec_b
        buf[z, f % 2] = new_fields[f]

    lane = lax.broadcasted_iota(jnp.int32, (size_x, size_y), 1)
    fields = [height[0, l] for l in range(levels)]
    fields += [wind[0, 0, l] for l in range(levels)]
    fields += [wind[0, 1, l] for l in range(levels)]
    fields += [moisture[0, l] for l in range(levels)]
    width = size_y // (4 * levels)
    half = width // 2
    pack = jnp.zeros((size_x, size_y), f32)
    for k in range(4 * levels):
        moved = pltpu.roll(fields[k], (width * k + half) % size_y, 1)
        pack = jnp.where(lane // width == k, moved, pack)
    packed[...] = pack

    pl.semaphore_wait(barrier, plane - 1 + members - 1)

    chunks = [spec_a, spec_b, state_0, state_1, state_2, state_3, coarse_all]
    relays = [relay_spec.at[0], relay_spec.at[1]]
    relays += [relay_state.at[l] for l in range(levels)] + [relay_coarse]

    def to_across(c):
        return pltpu.make_async_remote_copy(
            src_ref=chunks[c].at[z],
            dst_ref=chunks[c].at[z],
            send_sem=mem_send.at[c, 0],
            recv_sem=mem_recv.at[c, z],
            device_id=(across, ix, iy),
            device_id_type=MESH,
        )

    def to_near(c):
        return pltpu.make_async_remote_copy(
            src_ref=chunks[c].at[z],
            dst_ref=chunks[c].at[z],
            send_sem=mem_send.at[c, 1],
            recv_sem=mem_recv.at[c, z],
            device_id=(near, ix, iy),
            device_id_type=MESH,
        )

    def to_outward(c):
        return pltpu.make_async_remote_copy(
            src_ref=relays[c],
            dst_ref=chunks[c].at[z],
            send_sem=mem_send.at[c, 1],
            recv_sem=mem_recv.at[c, z],
            device_id=(outward, ix, iy),
            device_id_type=MESH,
        )

    def arrival(c, source):
        return pltpu.make_async_remote_copy(
            src_ref=chunks[c].at[source],
            dst_ref=chunks[c].at[source],
            send_sem=mem_send.at[c, 0],
            recv_sem=mem_recv.at[c, source],
            device_id=(across, ix, iy),
            device_id_type=MESH,
        )

    def send_own(c):
        to_across(c).start()

        @pl.when(outer)
        def _():
            to_near(c).start()

    send_own(0)

    def halo_jobs(start):
        for dx in (-1, 0, 1):
            for dy in (-1, 0, 1):
                if dx == 0 and dy == 0:
                    continue
                ok = jnp.bool_(True)
                if dx == -1:
                    ok = jnp.logical_and(ok, ix > 0)
                if dx == 1:
                    ok = jnp.logical_and(ok, ix < count_x - 1)
                if dy == -1:
                    ok = jnp.logical_and(ok, iy > 0)
                if dy == 1:
                    ok = jnp.logical_and(ok, iy < count_y - 1)
                sx = 0 if dx == -1 else 1
                sy = 0 if dy == -1 else 1
                rows = pl.ds(0, HALO) if dx == -1 else pl.ds(size_x - HALO, HALO)
                target = (z, ix + dx, iy + dy)

                def go(dx=dx, dy=dy, sx=sx, sy=sy, rows=rows, target=target):
                    if dy == 0:
                        pairs = [
                            (height.at[0, :, rows, :], rows_h.at[sx]),
                            (wind.at[0, :, :, rows, :], rows_w.at[sx]),
                            (moisture.at[0, :, rows, :], rows_q.at[sx]),
                        ]
                        base = 3 * sx
                    elif dx == 0:
                        pairs = [(packed, packed_in.at[sy])]
                        base = 6 + sy
                    else:
                        pairs = [(packed.at[rows, :], diag_in.at[sx, sy])]
                        base = 8 + 2 * sx + sy
                    for n, (src, dst) in enumerate(pairs):
                        copy = pltpu.make_async_remote_copy(
                            src_ref=src,
                            dst_ref=dst,
                            send_sem=halo_send.at[base + n],
                            recv_sem=halo_recv.at[base + n],
                            device_id=target,
                            device_id_type=MESH,
                        )
                        if start == "start":
                            copy.start()
                        elif start == "send":
                            copy.wait_send()
                        else:
                            copy.wait_recv()

                if start == "recv":
                    ok = jnp.bool_(True)
                    if dx == -1:
                        ok = jnp.logical_and(ok, ix < count_x - 1)
                    if dx == 1:
                        ok = jnp.logical_and(ok, ix > 0)
                    if dy == -1:
                        ok = jnp.logical_and(ok, iy < count_y - 1)
                    if dy == 1:
                        ok = jnp.logical_and(ok, iy > 0)
                pl.when(ok)(go)

    halo_jobs("start")

    low = jnp.concatenate(new_fields, axis=0).astype(jnp.bfloat16)
    fetch.wait()
    part = jnp.dot(low, basis_buf[...], preferred_element_type=f32)
    for g in range(count_x):
        rim_part[g] = part[g * share : (g + 1) * share]

    def rim_copy(step):
        _, px, py = plane_peer(step)
        return pltpu.make_async_remote_copy(
            src_ref=rim_part.at[px],
            dst_ref=rim_in.at[here],
            send_sem=rim_send.at[step],
            recv_sem=rim_recv.at[here],
            device_id=(z, px, py),
            device_id_type=MESH,
        )

    for step in range(1, plane):
        rim_copy(step).start()
    send_own(1)

    n_edge = edge_source.shape[1]
    table[...] = (
        (lax.broadcasted_iota(jnp.int32, (rim_points, n_edge), 0) == edge_source[...])
        .astype(f32)
        .astype(jnp.bfloat16)
    )
    row_table = (
        lax.broadcasted_iota(jnp.int32, (coarse_x, full_x), 0) == row_cell[...]
    ).astype(f32)
    row_count = jnp.sum(row_table, axis=1, keepdims=True)
    wide = lax.rem(
        lax.broadcasted_iota(jnp.int32, (levels * coarse_y, full_y), 0), coarse_y
    )
    col_table = (wide == col_cell[...]).astype(f32)
    col_count = lax.dot_general(
        jnp.ones((8, full_y), f32),
        col_table,
        (((1,), (1,)), ((), ())),
        preferred_element_type=f32,
    )[0:1]
    col_off = pl.multiple_of(iy * size_y, 128)
    row_off = pl.multiple_of(ix * size_x, 8)
    cells_here = col_cell[:, pl.ds(col_off, size_y)]
    wide_here = lax.broadcasted_iota(jnp.int32, (levels * coarse_y, size_y), 0)
    coarse_rows_buf[...] = jnp.zeros_like(coarse_rows_buf)

    total = rim_part[ix]
    for step in range(1, plane):
        other, px, py = plane_peer(step)
        pltpu.make_async_remote_copy(
            src_ref=rim_part.at[px],
            dst_ref=rim_in.at[other],
            send_sem=rim_send.at[step],
            recv_sem=rim_recv.at[other],
            device_id=(z, px, py),
            device_id_type=MESH,
        ).wait_recv()
        total = total + rim_in[other]
    rim_full[ix] = total

    def rimg_copy(step, source):
        return pltpu.make_async_remote_copy(
            src_ref=rim_full.at[source],
            dst_ref=rim_full.at[source],
            send_sem=rimg_send.at[step],
            recv_sem=rimg_recv.at[source],
            device_id=(z, lax.rem(ix + step, count_x), iy),
            device_id_type=MESH,
        )

    for step in range(1, count_x):
        rimg_copy(step, ix).start()

    halo_jobs("recv")
    lane2 = lax.broadcasted_iota(jnp.int32, (size_x + 2 * HALO, size_y), 1)
    take_next = lax.rem(lane2, width) >= half
    nxt = jnp.concatenate([packed_in[0], diag_in[0, 0], diag_in[1, 0]], axis=0)
    prv = jnp.concatenate([packed_in[1], diag_in[0, 1], diag_in[1, 1]], axis=0)
    mixed = jnp.where(take_next, nxt, prv)

    ext_x = size_x + 2 * HALO
    ext_y = 2 * size_y
    rpos = lax.broadcasted_iota(jnp.int32, (ext_x, ext_y), 0)
    cpos = lax.broadcasted_iota(jnp.int32, (ext_x, ext_y), 1)
    gx_pos = ix * size_x + jnp.where(rpos < size_x + HALO, rpos, rpos - ext_x)
    gy_pos = iy * size_y + jnp.where(cpos < size_y + size_y // 2, cpos, cpos - ext_y)
    inside = (gx_pos >= 0) & (gx_pos < full_x) & (gy_pos >= 0) & (gy_pos < full_y)
    at_west = gx_pos == -1
    at_east = gx_pos == full_x
    at_south = gy_pos == -1

    for step in range(1, count_x):
        rimg_copy(step, lax.rem(ix + step, count_x)).wait_recv()
    rim = jnp.concatenate([rim_full[g] for g in range(count_x)], axis=0)
    rim_hi = rim.astype(jnp.bfloat16)
    rim_lo = (rim - rim_hi.astype(f32)).astype(jnp.bfloat16)
    both = jnp.dot(
        jnp.concatenate([rim_hi, rim_lo], axis=0), table[...], preferred_element_type=f32
    )
    n_rows = 4 * levels
    edge = both[0:n_rows] + both[n_rows:]
    sides[...] = edge
    for s in range(2):
        first = 2 * full_y + s * full_x
        sides_t[s, HALO : HALO + full_x, :] = edge[:, first : first + full_x].T
        sides_t[s, 0:HALO, :] = jnp.zeros((HALO, n_rows), f32)
        sides_t[s, HALO + full_x :, :] = jnp.zeros((HALO, n_rows), f32)
    lane1 = lax.broadcasted_iota(jnp.int32, (n_rows, size_y), 1)

    def x_side(first):
        own = sides[:, pl.ds(pl.multiple_of(first + col_off, 128), size_y)]
        after = lax.rem(iy + 1, count_y) * size_y
        before = lax.rem(iy + count_y - 1, count_y) * size_y
        nxt_b = sides[:, pl.ds(pl.multiple_of(first + after, 128), size_y)]
        prv_b = sides[:, pl.ds(pl.multiple_of(first + before, 128), size_y)]
        return jnp.concatenate([own, jnp.where(lane1 < size_y // 2, nxt_b, prv_b)], axis=1)

    def y_side(s):
        body_rows = sides_t[s, pl.ds(pl.multiple_of(row_off + HALO, 8), size_x), :]
        above = sides_t[s, pl.ds(pl.multiple_of(row_off + HALO + size_x, 8), HALO), :]
        below = sides_t[s, pl.ds(row_off, HALO), :]
        return jnp.concatenate([body_rows, above, below], axis=0)

    west, east = x_side(0), x_side(full_y)
    south, north = y_side(0), y_side(1)

    states = [state_0, state_1, state_2, state_3]
    for l in range(levels):
        def extended(f, tile, above, below):
            k = f * levels + l
            left = jnp.concatenate([tile, above, below], axis=0)
            right = pltpu.roll(mixed, (size_y - (width * k + half)) % size_y, 1)
            return jnp.concatenate([left, right], axis=1)

        def outside(f):
            k = f * levels + l
            value = jnp.where(at_south, south[:, k : k + 1], north[:, k : k + 1])
            value = jnp.where(at_east, east[k : k + 1], value)
            return jnp.where(at_west, west[k : k + 1], value)

        def up(a):
            return pltpu.roll(a, ext_x - 1, 0)

        def down(a):
            return pltpu.roll(a, 1, 0)

        def right_of(a):
            return pltpu.roll(a, ext_y - 1, 1)

        def left_of(a):
            return pltpu.roll(a, 1, 1)

        bh, bu, bv, bq = outside(0), outside(1), outside(2), outside(3)
        h = extended(0, fields[l], rows_h[0, l], rows_h[1, l])
        u = extended(1, fields[levels + l], rows_w[0, 0, l], rows_w[1, 0, l])
        v = extended(2, fields[2 * levels + l], rows_w[0, 1, l], rows_w[1, 1, l])
        q = extended(3, fields[3 * levels + l], rows_q[0, l], rows_q[1, l])
        h = jnp.where(inside, h, bh)
        q = jnp.where(inside, q, bq)
        for substep in range(ACOUSTIC):
            u = u - acoustic_substep * (up(h) - down(h))
            v = v - acoustic_substep * (right_of(h) - left_of(h))
            u = jnp.where(inside, u, bu)
            v = jnp.where(inside, v, bv)
            h = h - acoustic_substep * ((up(u) - down(u)) + (right_of(v) - left_of(v)))
            h = jnp.where(inside, h, bh)
        flux = (
            jnp.maximum(u, 0.0) * (q - down(q)) + jnp.minimum(u, 0.0) * (up(q) - q)
        ) + (
            jnp.maximum(v, 0.0) * (q - left_of(q)) + jnp.minimum(v, 0.0) * (right_of(q) - q)
        )
        q = (q - drift_step * flux)[0:size_x, 0:size_y]
        states[l][z, 0] = h[0:size_x, 0:size_y]
        states[l][z, 1] = u[0:size_x, 0:size_y]
        states[l][z, 2] = v[0:size_x, 0:size_y]
        states[l][z, 3] = q
        send_own(2 + l)

        fallen = cond_rate[l] * jnp.maximum(q - saturation[l], 0.0)
        q_new = q - fallen
        spread = ((wide_here - l * coarse_y) == cells_here).astype(f32)
        summed = lax.dot_general(
            q_new,
            spread,
            (((1,), (1,)), ((), ())),
            precision=lax.Precision.HIGHEST,
            preferred_element_type=f32,
        )
        rows_here = pl.ds(row_off, size_x)
        coarse_rows_buf[rows_here, :] = coarse_rows_buf[rows_here, :] + summed

    coarse_part[...] = jnp.dot(
        row_table,
        coarse_rows_buf[...],
        precision=lax.Precision.HIGHEST,
        preferred_element_type=f32,
    )

    def crs_copy(step, source):
        _, px, py = plane_peer(step)
        return pltpu.make_async_remote_copy(
            src_ref=coarse_part,
            dst_ref=coarse_in.at[source],
            send_sem=crs_send.at[step],
            recv_sem=crs_recv.at[source],
            device_id=(z, px, py),
            device_id_type=MESH,
        )

    for step in range(1, plane):
        crs_copy(step, here).start()

    pick = ancestry[z]
    pick = jnp.where(z == 0, jnp.minimum(pick, 1), pick)
    pick = jnp.where(z == members - 1, jnp.maximum(pick, members - 2), pick)
    passed = jnp.where(
        z < 2, jnp.maximum(ancestry[0], 1), jnp.minimum(ancestry[members - 1], members - 2)
    )

    def pass_on(c):
        @pl.when(inner)
        def _():
            arrival(c, 0).wait_recv()
            arrival(c, members - 1).wait_recv()
            arrival(c, across).wait_recv()
            relays[c][...] = chunks[c][passed]
            to_outward(c).start()

    def settle(c):
        @pl.when(outer)
        def _():
            arrival(c, near).wait_recv()

        return chunks[c][pick]

    pass_on(0)
    pass_on(1)

    total = coarse_part[...]
    for step in range(1, plane):
        other, _, _ = plane_peer(step)
        crs_copy(step, other).wait_recv()
        total = total + coarse_in[other]
    coarse_all[z] = total / (row_count * col_count)
    send_own(6)

    for c in range(2):
        got = settle(c)
        coeffs_out[0, 2 * c] = got[0]
        coeffs_out[0, 2 * c + 1] = got[1]

    for l in range(levels):
        pass_on(2 + l)
    pass_on(6)

    rain = jnp.zeros((size_x, size_y), f32)
    for l in range(levels):
        got = settle(2 + l)
        height_out[0, l] = got[0]
        wind_out[0, 0, l] = got[1]
        wind_out[0, 1, l] = got[2]
        fallen = cond_rate[l] * jnp.maximum(got[3] - saturation[l], 0.0)
        moisture_out[0, l] = got[3] - fallen
        rain = rain + fallen
    rain_out[0] = rain
    got = settle(6)
    for l in range(levels):
        coarse_out[0, l] = got[:, l * coarse_y : (l + 1) * coarse_y]

    halo_jobs("send")
    for step in range(1, plane):
        rim_copy(step).wait_send()
        crs_copy(step, here).wait_send()
    for step in range(1, count_x):
        rimg_copy(step, ix).wait_send()
    for c in range(7):
        to_across(c).wait_send()

        @pl.when(outer)
        def _(c=c):
            to_near(c).wait_send()

        @pl.when(inner)
        def _(c=c):
            to_outward(c).wait_send()


def body(
    sizes,
    height,
    wind,
    moisture,
    coeffs,
    damping,
    vmix,
    basis,
    edge_source,
    row_cell,
    col_cell,
    cond_rate,
    saturation,
    ancestry,
):
    members, count_x, count_y = sizes
    plane = count_x * count_y
    _, levels, size_x, size_y = height.shape
    local_k = coeffs.shape[3]
    rim_points = basis.shape[1]
    full_x = row_cell.shape[0]
    full_y = col_cell.shape[0]
    n_edge = edge_source.shape[0]
    coarse_x, coarse_y = full_x // RATIO, full_y // RATIO
    share = 4 * levels // count_x
    rows = 4 * levels
    f32 = jnp.float32
    vmem = pl.BlockSpec(memory_space=pltpu.VMEM)
    smem = pl.BlockSpec(memory_space=pltpu.SMEM)
    dma = pltpu.SemaphoreType.DMA
    spec_chunk = (2, levels, local_k)
    state_chunk = (4, size_x, size_y)
    coarse_chunk = (coarse_x, levels * coarse_y)
    scratch = [
        pltpu.VMEM(basis.shape, basis.dtype),
        pltpu.VMEM((members, *spec_chunk), f32),
        pltpu.VMEM((members, *spec_chunk), f32),
        *[pltpu.VMEM((members, *state_chunk), f32) for _ in range(4)],
        pltpu.VMEM((members, *coarse_chunk), f32),
        pltpu.VMEM((2, *spec_chunk), f32),
        pltpu.VMEM((levels, *state_chunk), f32),
        pltpu.VMEM(coarse_chunk, f32),
        pltpu.VMEM((size_x, size_y), f32),
        pltpu.VMEM((2, size_x, size_y), f32),
        pltpu.VMEM((2, 2, HALO, size_y), f32),
        pltpu.VMEM((2, levels, HALO, size_y), f32),
        pltpu.VMEM((2, 2, levels, HALO, size_y), f32),
        pltpu.VMEM((2, levels, HALO, size_y), f32),
        pltpu.VMEM((count_x, share, rim_points), f32),
        pltpu.VMEM((plane, share, rim_points), f32),
        pltpu.VMEM((count_x, share, rim_points), f32),
        pltpu.VMEM((rim_points, n_edge), jnp.bfloat16),
        pltpu.VMEM((rows, n_edge), f32),
        pltpu.VMEM((2, full_x + 2 * HALO, rows), f32),
        pltpu.VMEM((full_x, levels * coarse_y), f32),
        pltpu.VMEM(coarse_chunk, f32),
        pltpu.VMEM((plane, *coarse_chunk), f32),
        dma,
        dma((12,)),
        dma((12,)),
        dma((plane,)),
        dma((plane,)),
        dma((count_x,)),
        dma((count_x,)),
        dma((plane,)),
        dma((plane,)),
        dma((7, 2)),
        dma((7, members)),
    ]
    outs = (
        jax.ShapeDtypeStruct(height.shape, f32),
        jax.ShapeDtypeStruct(wind.shape, f32),
        jax.ShapeDtypeStruct(moisture.shape, f32),
        jax.ShapeDtypeStruct((1, size_x, size_y), f32),
        jax.ShapeDtypeStruct((1, levels, coarse_x, coarse_y), f32),
        jax.ShapeDtypeStruct(coeffs.shape, f32),
    )
    return pl.pallas_call(
        functools.partial(kernel, sizes),
        out_shape=outs,
        in_specs=[
            vmem,
            vmem,
            vmem,
            vmem,
            vmem,
            vmem,
            pl.BlockSpec(memory_space=pl.ANY),
            vmem,
            vmem,
            vmem,
            smem,
            smem,
            smem,
        ],
        out_specs=(vmem,) * 6,
        scratch_shapes=scratch,
        compiler_params=pltpu.CompilerParams(
            collective_id=0, has_side_effects=True, vmem_limit_bytes=60 * 1024 * 1024
        ),
    )(
        height,
        wind,
        moisture,
        coeffs,
        damping.reshape(1, -1),
        vmix,
        basis,
        edge_source.reshape(1, -1),
        row_cell.reshape(1, -1),
        col_cell.reshape(1, -1),
        cond_rate,
        saturation,
        ancestry,
    )


def solution(mesh):
    sizes = (mesh.shape["mem"], mesh.shape["gx"], mesh.shape["gy"])
    in_specs = (
        P("mem", None, "gx", "gy"),
        P("mem", None, None, "gx", "gy"),
        P("mem", None, "gx", "gy"),
        P("mem", None, None, ("gx", "gy")),
        P(("gx", "gy")),
        P(),
        P(("gx", "gy"), None),
        P(),
        P(),
        P(),
        P(),
        P(),
        P(),
    )
    out_specs = (
        P("mem", None, "gx", "gy"),
        P("mem", None, None, "gx", "gy"),
        P("mem", None, "gx", "gy"),
        P("mem", "gx", "gy"),
        P("mem", None, None, None),
        P("mem", None, None, ("gx", "gy")),
    )
    return jax.shard_map(
        functools.partial(body, sizes),
        mesh=mesh,
        in_specs=in_specs,
        out_specs=out_specs,
        check_vma=False,
    )
```

time: 246 us -> 43.7 us (0.18)
  blocking collectives: 133 us -> 0 us
  starting transfers between devices: 52.2 us -> 0 us
  Pallas kernels: 0 us -> 32.5 us
  local copies, waits for them, and re-layouts: 37.8 us -> 10 us
  waiting for transfers between devices: 10.6 us -> 0 us
  other arithmetic: 5.81 us -> 0 us
  between operations: 3.52 us -> 0.64 us
  matrix products: 2.68 us -> 0 us
    all_gather x6 -> x0, blocking collectives: 87.9 us -> none  [the longest x1 17 us: body(): lax.all_gather(states[1], 'mem', axis=0, tiled=True)]
    ppermute x20 -> x0, starting transfers between devices: 52.2 us -> none  [the longest x10 39.2 us: extended(): lax.ppermute(lax.slice_in_dim(block, block.shape[dim] - width, None, axis...]
    psum x3 -> x0, blocking collectives: 44.8 us -> none  [the longest x1 25.8 us: body(): rim = lax.psum(rim_part, ('gx', 'gy'))]
    pallas_call x0 -> x1, Pallas kernels: none -> 32.5 us  [body(): pl.pallas_call(functools.partial(kernel, sizes), out_shape=outs, in_specs...]
    scatter x20 -> x0, local copies, waits for them, and re-layouts: 27.7 us -> none  [the longest x5 16.9 us: frame(): padded.at[:, :, 1:1 + size_x, 1 + size_y]]
    ppermute x20 -> x0, waiting for transfers between devices: 10.6 us -> none  [the longest x10 5.56 us: extended(): lax.ppermute(lax.slice_in_dim(block, 0, width, axis=dim), axis, backward)]
    unnamed x22 -> x6, local copies, waits for them, and re-layouts: 0.17 us -> 8.78 us
    dynamic_slice x9 -> x0, local copies, waits for them, and re-layouts: 5.22 us -> none  [the longest x6 3.82 us: body(): lax.dynamic_index_in_dim(whole, source, 0, keepdims=True)]
  transfers between devices with their start and end apart: 20 -> 0, of which waited for: 8 -> 0; matrix products, arithmetic and copies ran while one was open for 9% -> 0% of each run, Pallas kernels for 0% -> 0%
where the time goes in v1:
time: 43.7 us; the launch traced here: 43.2 us
  Pallas kernels  32.5 us (74%)
  local copies, waits for them, and re-layouts  10 us (23%)
  between operations  0.64 us (1%)
    pallas_call x1, Pallas kernels, body(): pl.pallas_call(functools.partial(kernel, sizes), out_shape=outs, in_specs...  32.5 us
    unnamed x6, local copies, waits for them, and re-layouts  8.78 us
    reshape x1, local copies, waits for them, and re-layouts, body(): edge_source.reshape(1, -1)  1.27 us

profile of v1, /device:TPU:0, one launch (start us, length us, event | category | flops | bytes accessed | tf_op | source)
XLA Modules:
  0.0 43.2 jit_solution(10240379728984504133)
XLA Ops:
  0.6 1.3 %reshape.25.edge_source = s32[1,768]{1,0:T(1,128)} reshape(s32[768]{0:T(1024)} %param.20) | data formatting | bytes 6144 | tf_op jit(solution)/shard_map/reshape | solution.py:660
  1.9 32.5 %shard_map.172 = (f32[1,4,32,128]{3,2,1,0:T(8,128)}, f32[1,2,4,32,128]{4,3,2,1,0:T(8,128)}, f32[1,4,32,128]{3,2,1,0:T(8,128)}, f32[1,32,128]{2,1,0:T(8,128)}, f3...) custom-call(f32[1,4,32,128]{3,2,1,0:T(8,128)} %height.1, f32[1,2,4,32,128]{4,3,2,1,0:T(8,128)} %wind.1, ...), custom_call_target="tpu_custom_call" | custom-call | tf_op jit(solution)/shard_map/pallas_call | solution.py:629
  34.5 1.5 %copy.25 = f32[1,4,32,128]{3,2,1,0:T(8,128)} copy(f32[1,4,32,128]{3,2,1,0:T(8,128)} %get-tuple-element.12) | data formatting | bytes 131072
  35.9 1.6 %copy.26 = f32[1,2,4,32,128]{4,3,2,1,0:T(8,128)} copy(f32[1,2,4,32,128]{4,3,2,1,0:T(8,128)} %get-tuple-element.13) | data formatting | bytes 262144
  37.5 1.5 %copy.27 = f32[1,4,32,128]{3,2,1,0:T(8,128)} copy(f32[1,4,32,128]{3,2,1,0:T(8,128)} %get-tuple-element.14) | data formatting | bytes 131072
  39.0 1.3 %copy.28 = f32[1,32,128]{2,1,0:T(8,128)} copy(f32[1,32,128]{2,1,0:T(8,128)} %get-tuple-element.15) | data formatting | bytes 32768
  40.3 1.4 %copy.29 = f32[1,4,16,32]{3,2,1,0:T(8,128)} copy(f32[1,4,16,32]{3,2,1,0:T(8,128)} %get-tuple-element.16) | data formatting | bytes 16384
  41.7 1.6 %copy.30 = f32[1,4,4,2048]{3,2,1,0:T(4,128)} copy(f32[1,4,4,2048]{3,2,1,0:T(4,128)} %get-tuple-element.17) | data formatting | bytes 262144

commit v2 on v1

--- a/solution.py
+++ b/solution.py
@@ -38,7 +38,7 @@
     rain_out,
     coarse_out,
     coeffs_out,
-    basis_buf,
+    ready,
     spec_a,
     spec_b,
     state_0,
@@ -64,7 +64,6 @@
     coarse_rows_buf,
     coarse_part,
     coarse_in,
-    basis_sem,
     halo_send,
     halo_recv,
     rim_send,
@@ -99,9 +98,6 @@
     near = jnp.where(z < 2, 1, 2)
     outward = jnp.where(z < 2, 0, 3)
 
-    fetch = pltpu.make_async_copy(basis, basis_buf, basis_sem)
-    fetch.start()
-
     def plane_peer(step):
         other = lax.rem(here + step, plane)
         return other, other // count_y, lax.rem(other, count_y)
@@ -118,6 +114,7 @@
             device_id_type=MESH,
         )
 
+    ready(3, 4, 5)
     new_fields = []
     for f in range(4):
         c = coeffs[0, f]
@@ -129,6 +126,7 @@
         buf = spec_a if f < 2 else spec_b
         buf[z, f % 2] = new_fields[f]
 
+    ready(0, 1, 2)
     lane = lax.broadcasted_iota(jnp.int32, (size_x, size_y), 1)
     fields = [height[0, l] for l in range(levels)]
     fields += [wind[0, 0, l] for l in range(levels)]
@@ -261,8 +259,8 @@
     halo_jobs("start")
 
     low = jnp.concatenate(new_fields, axis=0).astype(jnp.bfloat16)
-    fetch.wait()
-    part = jnp.dot(low, basis_buf[...], preferred_element_type=f32)
+    ready(6)
+    part = jnp.dot(low, basis[...], preferred_element_type=f32)
     for g in range(count_x):
         rim_part[g] = part[g * share : (g + 1) * share]
 
@@ -281,9 +279,11 @@
         rim_copy(step).start()
     send_own(1)
 
-    n_edge = edge_source.shape[1]
+    ready(7, 8, 9, 10, 11, 12)
+    n_edge = edge_source.shape[0]
     table[...] = (
-        (lax.broadcasted_iota(jnp.int32, (rim_points, n_edge), 0) == edge_source[...])
+        (lax.broadcasted_iota(jnp.int32, (rim_points, n_edge), 0)
+         == edge_source[...].reshape(1, n_edge))
         .astype(f32)
         .astype(jnp.bfloat16)
     )
@@ -546,6 +546,29 @@
         @pl.when(inner)
         def _(c=c):
             to_outward(c).wait_send()
+
+
+def staged_kernel(sizes, *refs):
+    sources, outs, held = refs[:13], refs[13:19], refs[19:32]
+    sems, rest = refs[-1], refs[32:-1]
+    copies = [pltpu.make_async_copy(sources[n], held[n], sems.at[n]) for n in range(13)]
+    for n in (3, 4, 5, 0, 1, 2, 6, 7, 8, 9, 10, 11, 12):
+        copies[n].start()
+
+    def ready(*which):
+        for n in which:
+            copies[n].wait()
+
+    kernel(sizes, *held, *outs, ready, *rest)
+
+
+def write_out(*refs):
+    sems = refs[12]
+    copies = [pltpu.make_async_copy(refs[n], refs[6 + n], sems.at[n]) for n in range(6)]
+    for copy in copies:
+        copy.start()
+    for copy in copies:
+        copy.wait()
 
 
 def body(
@@ -577,13 +600,28 @@
     rows = 4 * levels
     f32 = jnp.float32
     vmem = pl.BlockSpec(memory_space=pltpu.VMEM)
-    smem = pl.BlockSpec(memory_space=pltpu.SMEM)
     dma = pltpu.SemaphoreType.DMA
     spec_chunk = (2, levels, local_k)
     state_chunk = (4, size_x, size_y)
     coarse_chunk = (coarse_x, levels * coarse_y)
+    operands = (
+        height,
+        wind,
+        moisture,
+        coeffs,
+        damping.reshape(1, -1),
+        vmix,
+        basis,
+        edge_source,
+        row_cell.reshape(1, -1),
+        col_cell.reshape(1, -1),
+        cond_rate,
+        saturation,
+        ancestry,
+    )
     scratch = [
-        pltpu.VMEM(basis.shape, basis.dtype),
+        *[pltpu.VMEM(a.shape, a.dtype) for a in operands[:10]],
+        *[pltpu.SMEM(a.shape, a.dtype) for a in operands[10:]],
         pltpu.VMEM((members, *spec_chunk), f32),
         pltpu.VMEM((members, *spec_chunk), f32),
         *[pltpu.VMEM((members, *state_chunk), f32) for _ in range(4)],
@@ -606,7 +644,6 @@
         pltpu.VMEM((full_x, levels * coarse_y), f32),
         pltpu.VMEM(coarse_chunk, f32),
         pltpu.VMEM((plane, *coarse_chunk), f32),
-        dma,
         dma((12,)),
         dma((12,)),
         dma((plane,)),
@@ -617,53 +654,34 @@
         dma((plane,)),
         dma((7, 2)),
         dma((7, members)),
+        dma((13,)),
     ]
     outs = (
-        jax.ShapeDtypeStruct(height.shape, f32),
-        jax.ShapeDtypeStruct(wind.shape, f32),
-        jax.ShapeDtypeStruct(moisture.shape, f32),
-        jax.ShapeDtypeStruct((1, size_x, size_y), f32),
-        jax.ShapeDtypeStruct((1, levels, coarse_x, coarse_y), f32),
-        jax.ShapeDtypeStruct(coeffs.shape, f32),
-    )
-    return pl.pallas_call(
-        functools.partial(kernel, sizes),
+        pltpu.VMEM(height.shape, f32),
+        pltpu.VMEM(wind.shape, f32),
+        pltpu.VMEM(moisture.shape, f32),
+        pltpu.VMEM((1, size_x, size_y), f32),
+        pltpu.VMEM((1, levels, coarse_x, coarse_y), f32),
+        pltpu.VMEM(coeffs.shape, f32),
+    )
+    results = pl.pallas_call(
+        functools.partial(staged_kernel, sizes),
         out_shape=outs,
-        in_specs=[
-            vmem,
-            vmem,
-            vmem,
-            vmem,
-            vmem,
-            vmem,
-            pl.BlockSpec(memory_space=pl.ANY),
-            vmem,
-            vmem,
-            vmem,
-            smem,
-            smem,
-            smem,
-        ],
+        in_specs=[pl.BlockSpec(memory_space=pltpu.HBM)] * 13,
         out_specs=(vmem,) * 6,
         scratch_shapes=scratch,
         compiler_params=pltpu.CompilerParams(
-            collective_id=0, has_side_effects=True, vmem_limit_bytes=60 * 1024 * 1024
+            collective_id=0, has_side_effects=True, vmem_limit_bytes=36 * 1024 * 1024
         ),
-    )(
-        height,
-        wind,
-        moisture,
-        coeffs,
-        damping.reshape(1, -1),
-        vmix,
-        basis,
-        edge_source.reshape(1, -1),
-        row_cell.reshape(1, -1),
-        col_cell.reshape(1, -1),
-        cond_rate,
-        saturation,
-        ancestry,
-    )
+    )(*[pltpu.with_memory_space_constraint(a, pltpu.HBM) for a in operands])
+    return pl.pallas_call(
+        write_out,
+        out_shape=tuple(jax.ShapeDtypeStruct(r.shape, f32) for r in results),
+        in_specs=[vmem] * 6,
+        out_specs=(pl.BlockSpec(memory_space=pl.ANY),) * 6,
+        scratch_shapes=[dma((6,))],
+        compiler_params=pltpu.CompilerParams(vmem_limit_bytes=8 * 1024 * 1024),
+    )(*results)
 
 
 def solution(mesh):

time: 43.7 us -> 32.5 us (0.74)
  local copies, waits for them, and re-layouts: 10 us -> 0 us
  Pallas kernels: 32.5 us -> 31.7 us
    unnamed x6 -> x0, local copies, waits for them, and re-layouts: 8.78 us -> none
    reshape x1 -> x0, local copies, waits for them, and re-layouts: 1.27 us -> none  [body(): edge_source.reshape(1, -1)]
    pallas_call x1 -> x2, Pallas kernels: 32.5 us -> 31.7 us  [the longest x1 30.9 us: body(): pl.pallas_call(functools.partial(staged_kernel, sizes), out_shape=outs, i...]
where the time goes in v2:
time: 32.5 us; the launch traced here: 32.3 us
  Pallas kernels  31.7 us (98%)
  between operations  0.65 us (2%)
    pallas_call x1, Pallas kernels, body(): pl.pallas_call(functools.partial(staged_kernel, sizes), out_shape=outs, i...  30.9 us
    pallas_call x1, Pallas kernels, body(): pl.pallas_call(write_out, out_shape=tuple((jax.ShapeDtypeStruct(r.shape,...  0.81 us

profile of v2, /device:TPU:0, one launch (start us, length us, event | category | flops | bytes accessed | tf_op | source)
XLA Modules:
  0.0 32.3 jit_solution(12172062566122946398)
XLA Ops:
  0.6 30.9 %shard_map.172 = (f32[1,4,32,128]{3,2,1,0:T(8,128)S(1)}, f32[1,2,4,32,128]{4,3,2,1,0:T(8,128)S(1)}, f32[1,4,32,128]{3,2,1,0:T(8,128)S(1)}, f32[1,32,128]{2,1,0:T...) custom-call(f32[1,4,32,128]{3,2,1,0:T(8,128)} %refs_0_.1, f32[1,2,4,32,128]{4,3,2,1,0:T(8,128)} %refs_1_.1, ...), custom_call_target="tpu_custom_call" | custom-call | tf_op jit(solution)/shard_map/pallas_call | solution.py:667
  31.5 0.8 %shard_map.173 = (f32[1,4,32,128]{3,2,1,0:T(8,128)}, f32[1,2,4,32,128]{4,3,2,1,0:T(8,128)}, f32[1,4,32,128]{3,2,1,0:T(8,128)}, f32[1,32,128]{2,1,0:T(8,128)}, f3...) custom-call(f32[1,4,32,128]{3,2,1,0:T(8,128)S(1)} %get-tuple-element.12.refs_0_, ...), custom_call_target="tpu_custom_call" | custom-call | tf_op jit(solution)/shard_map/pallas_call | solution.py:677
